TPU v7x, 32 devices: a whole 2x2x4 slice. The times are simulated.
32 devices in a mesh: user: 4 (over x, core), item: 8 (over z, y).
Axes of the slice: x: 2, y: 2, z: 4, core: 2. Of those that a mesh axis runs over, the one named last changes fastest.
Arguments:
- item_feats: bfloat16 [131072, 1024], P(('user', 'item')), may hold values from -30 to 30
- first_weight: bfloat16 [1024, 512], replicated, may hold values from -0.1875 to 0.1875
- second_weight: bfloat16 [512, 256], replicated, may hold values from -0.25 to 0.25
- counts: int32 [131072], P(('user', 'item')), may hold values from 1 to 245760
- user_embed: bfloat16 [8192, 256], P(('user', 'item')), may hold values from -1 to 1
- list_owner: int32 [4096, 1], P(('user', 'item')), may hold values from 0 to 31, as said below
- list_slot: int32 [4096], P(('user', 'item')), may hold values from 0 to 31
- positive: int32 [8192], P(('user', 'item')), may hold values from 0 to 2047
Outputs:
- user_loss: float32 [8192], P(('user', 'item'))
- user_gradient: float32 [8192, 256], P(('user', 'item'))
- first_gradient: float32 [1024, 512], replicated
- second_gradient: float32 [512, 256], replicated
Inputs may be any that keep to these rules, and one draw needn't show every extreme that they name: `list_owner`: the rows of one device (128 of them, an aligned block) name any one owner at most 8 times; in every draw one owner is named exactly 8 times in the rows of every device.
All inputs are finite; a program needn't handle non-finite values.
Results may differ from a plain program's by a relative error of at most 0.0064.
Values may be sent and summed in bfloat16 or wider, within the bound.
No kernel may reach another device: no remote copies, remote signals or barrier semaphores. Data moves between devices by JAX's collectives and lax.ppermute only.
A program may use at most 192 MiB of HBM per device.

v0:
```python
import jax
import jax.numpy as jnp
from jax import lax
from jax.sharding import PartitionSpec as P

BLK = 128
NQ = 8
QB = 16
LOGIT_SCALE = 20.0
LOSS_SCALE = 4096.0
NORM_EPSILON = 1e-06


def body(
    item_feats, first_weight, second_weight, counts, user_embed, list_owner, list_slot, positive
):
    devices = lax.axis_size(("user", "item"))
    item_rows = item_feats.shape[0]
    own_blocks = item_rows // BLK
    user_rows = user_embed.shape[0]
    requests = list_slot.shape[0]
    capacity = 2 * requests // devices
    group_size = user_rows // NQ
    all_users = user_rows * devices
    linear_one = jnp.dot(item_feats, first_weight, preferred_element_type=jnp.float32)
    hidden = jnp.maximum(linear_one, 0.0).astype(jnp.bfloat16)
    tower_out = jnp.dot(hidden, second_weight, preferred_element_type=jnp.float32)
    item_norm = lax.rsqrt(jnp.sum(tower_out * tower_out, axis=1, keepdims=True) + NORM_EPSILON)
    vector_blocks = (tower_out * item_norm).astype(jnp.bfloat16).reshape(own_blocks, BLK, -1)
    log_blocks = jnp.log(counts.astype(jnp.float32)).astype(jnp.bfloat16).reshape(own_blocks, BLK)
    user_float = user_embed.astype(jnp.float32)
    user_norm = lax.rsqrt(jnp.sum(user_float * user_float, axis=1, keepdims=True) + NORM_EPSILON)
    user_vector = (user_float * user_norm).astype(jnp.bfloat16)
    group_users = user_vector.reshape(NQ, group_size, -1)
    group_pos = positive.reshape(NQ, group_size)
    owners = list_owner[:, 0]
    one_hot = (owners[:, None] == jnp.arange(devices, dtype=jnp.int32)[None, :]).astype(jnp.int32)
    earlier = jnp.cumsum(one_hot, axis=0) - one_hot
    position = owners * capacity + jnp.sum(earlier * one_hot, axis=1)
    send_slots = (
        jnp.zeros((devices * capacity,), jnp.int32)
        .at[position]
        .set(list_slot)
        .reshape(devices, capacity)
    )
    index_rows = jnp.arange(requests, dtype=jnp.int32)
    list_index = index_rows // QB
    offset = index_rows % QB * BLK
    local_pos = group_pos[list_index] - offset[:, None]
    local_pos = jnp.where((local_pos >= 0) & (local_pos < BLK), local_pos, -1)
    slot_users = (
        jnp.zeros((devices * capacity, group_size, group_users.shape[2]), jnp.bfloat16)
        .at[position]
        .set(group_users[list_index])
    )
    slot_pos = jnp.full((devices * capacity, group_size), -1, jnp.int32).at[position].set(local_pos)
    slot_ids, pos_in = (
        lax.all_to_all(send_slots, ("user", "item"), split_axis=0, concat_axis=0, tiled=True),
        lax.all_to_all(
            slot_pos.reshape(devices, capacity, group_size),
            ("user", "item"),
            split_axis=0,
            concat_axis=0,
            tiled=True,
        ),
    )
    users_in = lax.all_to_all(
        slot_users.reshape(devices, capacity, group_size, -1),
        ("user", "item"),
        split_axis=0,
        concat_axis=0,
        tiled=True,
    )
    blocks_in = vector_blocks[slot_ids]
    logs_in = log_blocks[slot_ids].astype(jnp.float32)
    scores = (
        LOGIT_SCALE
        * jnp.einsum("nkue,nkbe->nkub", users_in, blocks_in, preferred_element_type=jnp.float32)
        - logs_in[:, :, None, :]
    )
    exp_scores = jnp.exp(scores)
    is_positive = jnp.arange(BLK, dtype=jnp.int32)[None, None, None, :] == pos_in[:, :, :, None]
    part_totals = jnp.sum(exp_scores, axis=3)
    part_pos = jnp.sum(jnp.where(is_positive, scores, 0.0), axis=3)
    back_totals, back_pos = (
        lax.all_to_all(part_totals, ("user", "item"), split_axis=0, concat_axis=0, tiled=True),
        lax.all_to_all(part_pos, ("user", "item"), split_axis=0, concat_axis=0, tiled=True),
    )
    totals = (
        back_totals.reshape(devices * capacity, group_size)[position]
        .reshape(NQ, QB, group_size)
        .sum(axis=1)
    )
    pos_score = (
        back_pos.reshape(devices * capacity, group_size)[position]
        .reshape(NQ, QB, group_size)
        .sum(axis=1)
    )
    user_loss = jnp.log(totals) - pos_score
    slot_totals = (
        jnp.ones((devices * capacity, group_size), jnp.float32).at[position].set(totals[list_index])
    )
    totals_in = lax.all_to_all(
        slot_totals.reshape(devices, capacity, group_size),
        ("user", "item"),
        split_axis=0,
        concat_axis=0,
        tiled=True,
    )
    score_grad = (
        LOSS_SCALE
        / all_users
        * (exp_scores / totals_in[:, :, :, None] - is_positive.astype(jnp.float32))
    ).astype(jnp.bfloat16)
    returned = (
        LOGIT_SCALE
        * jnp.einsum("nkub,nkue->nkbe", score_grad, users_in, preferred_element_type=jnp.float32)
    ).astype(jnp.bfloat16)
    vector_parts = LOGIT_SCALE * jnp.einsum(
        "nkub,nkbe->nkue", score_grad, blocks_in, preferred_element_type=jnp.float32
    )
    parts_back = lax.all_to_all(
        vector_parts, ("user", "item"), split_axis=0, concat_axis=0, tiled=True
    )
    vector_grad = (
        parts_back.reshape(devices * capacity, group_size, -1)[position]
        .reshape(NQ, QB, group_size, -1)
        .sum(axis=1)
    )
    flat_ids = slot_ids.reshape(-1)
    selector = (jnp.arange(own_blocks, dtype=jnp.int32)[:, None] == flat_ids[None, :]).astype(
        jnp.bfloat16
    )
    item_gradient = jnp.dot(
        selector, returned.reshape(devices * capacity, -1), preferred_element_type=jnp.float32
    ).reshape(item_rows, -1)
    projection = jnp.sum(tower_out * item_gradient, axis=1, keepdims=True)
    out_gradient = (
        item_gradient * item_norm - tower_out * (projection * item_norm * item_norm * item_norm)
    ).astype(jnp.bfloat16)
    second_gradient = jnp.dot(hidden.T, out_gradient, preferred_element_type=jnp.float32)
    act_gradient = jnp.where(
        hidden > 0, jnp.dot(out_gradient, second_weight.T, preferred_element_type=jnp.float32), 0.0
    ).astype(jnp.bfloat16)
    first_gradient = jnp.dot(item_feats.T, act_gradient, preferred_element_type=jnp.float32)
    first_gradient, second_gradient = lax.psum((first_gradient, second_gradient), ("user", "item"))
    vector_grad = vector_grad.reshape(user_rows, -1)
    user_projection = jnp.sum(user_float * vector_grad, axis=1, keepdims=True)
    user_gradient = vector_grad * user_norm - user_float * (
        user_projection * user_norm * user_norm * user_norm
    )
    return (user_loss.reshape(user_rows), user_gradient, first_gradient, second_gradient)


def solution(mesh):
    return jax.shard_map(
        body,
        mesh=mesh,
        in_specs=(
            P(("user", "item"), None),
            P(),
            P(),
            P(("user", "item")),
            P(("user", "item"), None),
            P(("user", "item"), None),
            P(("user", "item")),
            P(("user", "item")),
        ),
        out_specs=(P(("user", "item")), P(("user", "item"), None), P(), P()),
        check_vma=False,
    )
```

profile of v0, /device:TPU:0, one launch (start us, length us, event | category | flops | bytes accessed | tf_op | source)
XLA Modules:
  0.0 490.5 jit_solution(11775205947933808178)
XLA Ops:
  7.2 0.8 fusion.13
  8.0 0.2 reduce_window_sum.11
  8.2 0.8 select_reduce_fusion.1
  9.0 0.7 fusion.27
  9.7 1.1 scatter_custom_fusion.1
  10.8 0.7 all_to_all.27
  11.5 7.3 %all-to-all-start.1 = ((s32[32,1,8]{2,1,0:T(1,128)}), s32[32,1,8]{2,1,0:T(1,128)S(1)}, u32[]{:S(2)}, u32[]{:S(2)}) async-start(s32[32,1,8]{2,1,0:T(1,128)} %bitcast.7), calls=%async_computation.1 | async-start | bytes 32768 | tf_op jit(solution)/shard_map/all_to_all | solution.py:58
  18.8 1.0 fusion.3
  19.9 0.8 reshape.192
  20.6 1.0 scatter_custom_fusion.2
  21.7 0.7 reshape.328
  22.4 3.4 all-to-all-done.1
  25.8 2.6 all-to-all-start.3
  28.4 1.0 fusion.4
  29.4 0.7 gather_fusion
  30.1 2.5 broadcast_in_dim.16
  32.6 15.7 %scatter_fusion = bf16[256,32,256]{2,1,0:T(8,128)(2,1)} fusion(bf16[256,32,256]{2,1,0:T(8,128)(2,1)} %broadcast_in_dim.16, s32[128]{0:T(128)S(1)} %fusion.27, bf16[128,32,256]{2,1,0:T(8,128)(2,1)S(1)} %gather_fusion), kind=kCustom, calls=%fused_computation.8 | custom fusion | bytes 6291968 | tf_op jit(solution)/shard_map/scatter | solution.py:54
  48.3 6.0 %all-to-all-start = ((bf16[32,8,32,256]{3,2,1,0:T(8,128)(2,1)}), bf16[32,8,32,256]{3,2,1,0:T(8,128)(2,1)}, u32[]{:S(2)}, u32[]{:S(2)}) async-start(bf16[32,8,32,256]{3,2,1,0:T(8,128)(2,1)} %bitcast.67), calls=%async_computation | async-start | bytes 8388608 | tf_op jit(solution)/shard_map/all_to_all | solution.py:67
  54.3 8.2 %maximum_convert_fusion = bf16[4096,512]{1,0:T(8,128)(2,1)S(1)} fusion(bf16[4096,1024]{1,0:T(8,128)(2,1)} %param.8, bf16[1024,512]{1,0:T(8,128)(2,1)S(1)} %copy-done), kind=kOutput, calls=%fused_computation.15 | convolution fusion | flops 4299161600 | bytes 13631488 | tf_op jit(solution)/shard_map/dot_general | solution.py:25
  62.5 1.3 multiply_reduce_fusion.1
  63.8 0.7 copy-done.5
  64.6 1.9 copy-done.2
  66.5 0.7 multiply_convert_fusion.2
  67.3 0.9 gather_fusion.2
  68.2 9.4 %gather_fusion.1 = bf16[256,128,256]{2,1,0:T(8,128)(2,1)} fusion(bf16[32,128,256]{2,1,0:T(8,128)(2,1)S(1)} %bitcast.62, s32[1024]{0:T(1024)S(1)} %pad_clamp_fusion.1), kind=kCustom, calls=%fused_computation.1 | custom fusion | bytes 33555456 | tf_op jit(solution)/shard_map/gather | solution.py:74
  77.5 0.5 broadcast.184
  78.1 0.7 reduce.4
  78.9 71.4 %all-to-all-done = bf16[32,8,32,256]{3,2,1,0:T(8,128)(2,1)} async-done(((bf16[32,8,32,256]{3,2,1,0:T(8,128)(2,1)}), bf16[32,8,32,256]{3,2,1,0:T(8,128)(2,1)}, u32[]{:S(2)}, u32[]{:S(2)}) %all-to-all-start) | async-done | bytes 4194336 | tf_op jit(solution)/shard_map/all_to_all | solution.py:67
  150.2 11.4 %exponential_reduce_fusion = (f32[32,8,32]{2,1,0:T(8,128)S(1)}, f32[32,8,32]{2,1,0:T(8,128)S(1)}, f32[32,8,32,128]{3,2,1,0:T(8,128)}) fusion(f32[32,8,128]{2,1,0:T(8,128)S(1)} %bitcast_convert_fusion, s32[32,8,32]{2,1,0:T(8,128)S(1)} %reshape.329, bf16[32,8,32,256]{3,2,1,0:T(8,128)(2,1)} %all-to-all-done, bf16[32,8,128,256]{3,2,1,0:T(8,128)(2,1)} %bitcast.63), kind=kOutput, calls=%fused_computation.26 | convolution fusion | flops 543145984 | bytes 25395200 | tf_op jit(solution)/shard_map/nkue,nkbe->nkub/dot_general | solution.py:78
  161.6 0.7 reshape.330
  162.3 2.6 all-to-all-start.4
  164.9 0.7 reshape.332
  165.7 6.5 %all-to-all-done.4 = f32[32,1,256]{2,1,0:T(1,128)S(1)} async-done(((f32[32,1,256]{2,1,0:T(1,128)}), f32[32,1,256]{2,1,0:T(1,128)S(1)}, u32[]{:S(2)}, u32[]{:S(2)}) %all-to-all-start.4) | async-done | bytes 32800 | tf_op jit(solution)/shard_map/all_to_all | solution.py:87
  172.1 2.7 all-to-all-start.2
  174.9 0.5 broadcast.185
  175.4 0.7 reduce.5
  176.2 5.8 %all-to-all-done.2 = f32[32,1,256]{2,1,0:T(1,128)S(1)} async-done(((f32[32,1,256]{2,1,0:T(1,128)}), f32[32,1,256]{2,1,0:T(1,128)S(1)}, u32[]{:S(2)}, u32[]{:S(2)}) %all-to-all-start.2) | async-done | bytes 32800 | tf_op jit(solution)/shard_map/all_to_all | solution.py:86
  182.0 0.7 reduce.6
  182.9 0.7 gather_fusion.4
  183.5 0.6 gather_fusion.3
  184.2 1.0 scatter_custom_fusion.3
  185.3 8.9 %all_to_all.42 = f32[32,1,256]{2,1,0:T(1,128)S(1)} all-to-all(f32[32,1,256]{2,1,0:T(1,128)S(1)} %reshape.334), channel_id=1, replica_groups=mesh['user'=4,'item'=8] {'user','item'}, dimensions={0} | all-to-all | bytes 65536 | tf_op jit(solution)/shard_map/all_to_all | solution.py:103
  194.2 0.7 reduce.7
  195.0 11.7 %broadcast_multiply_fusion = f32[32,8,32,256]{3,2,1,0:T(8,128)} fusion(bf16[32,8,128,256]{3,2,1,0:T(8,128)(2,1)} %bitcast.64, f32[32,8,32,128]{3,2,1,0:T(8,128)} %get-tuple-element.22, f32[32,8,32]{2,1,0:T(8,128)S(1)} %reshape.335, s32[32,8,32]{2,1,0:T(8,128)S(1)} %reshape.329, f32[32,8,128]{2,1,0:T(8,128)S(1)} %bitcast_convert_fusion), kind=kOutput, calls=%fused_computation.19 | convolution fusion | flops 547356672 | bytes 29556736 | tf_op jit(solution)/shard_map/nkub,nkbe->nkue/dot_general | solution.py:119
  206.7 3.7 all-to-all-start.6
  210.4 0.5 broadcast.183
  210.9 0.7 reduce.3
  211.7 13.0 %fusion = bf16[32,8,128,256]{3,2,1,0:T(8,128)(2,1)} fusion(bf16[32,8,32,256]{3,2,1,0:T(8,128)(2,1)} %all-to-all-done, f32[32,8,32,128]{3,2,1,0:T(8,128)} %get-tuple-element.22, f32[32,8,32]{2,1,0:T(8,128)S(1)} %reshape.335, s32[32,8,32]{2,1,0:T(8,128)S(1)} %reshape.329, f32[32,8,128]{2,1,0:T(8,128)S(1)} %bitcast_convert_fusion), kind=kOutput, calls=%fused_computation.13 | convolution fusion | flops 562036736 | bytes 25362432 | tf_op jit(solution)/shard_map/nkub,nkue->nkbe/dot_general | solution.py:117
  224.7 15.8 %copy.16 = bf16[32,8,128,256]{3,1,2,0:T(8,128)(2,1)S(1)} copy(bf16[32,8,128,256]{3,2,1,0:T(8,128)(2,1)} %fusion) | data formatting | bytes 33554432
  240.5 4.8 fusion.22
  245.3 4.9 reshape.201
  250.2 4.2 multiply_reduce_fusion
  254.4 0.4 copy-done.3
  254.8 1.3 copy-done.4
  256.1 2.4 subtract_convert_fusion
  258.5 2.1 fusion.33
  260.6 11.6 %fusion.2 = f32[1024,512]{0,1:T(8,128)} fusion(bf16[4096,1024]{1,0:T(8,128)(2,1)} %param.8, bf16[4096,512]{1,0:T(8,128)(2,1)} %copy-done.5, bf16[4096,256]{1,0:T(8,128)(2,1)S(1)} %subtract_convert_fusion, bf16[512,256]{1,0:T(8,128)(2,1)S(1)} %copy-done.9), kind=kOutput, calls=%fused_computation.28 | convolution fusion | flops 5375000576 | bytes 17039360 | tf_op jit(solution)/shard_map/dot_general | solution.py:145
  272.2 0.6 sub.52
  272.9 197.3 %all-reduce.3.cloned.1.call-done = (f32[1024,512]{0,1:T(8,128)}, f32[512,256]{1,0:T(8,128)}) async-done(((f32[1024,512]{0,1:T(8,128)}, f32[512,256]{1,0:T(8,128)}), (f32[1024,512]{0,1:T(8,128)}, f32[512,256]{1,0:T(8,128)})) %all-reduce.3.cloned.1.call-update) | async-done | bytes 2621456 | tf_op jit(solution)/shard_map/psum | solution.py:146
  470.2 2.9 copy.15
  473.1 6.2 %gather_fusion.5 = f32[128,32,256]{2,1,0:T(8,128)} fusion(f32[256,32,256]{2,1,0:T(8,128)} %bitcast.18, s32[1024]{0:T(1024)S(1)} %pad_clamp_fusion), kind=kCustom, calls=%fused_computation.7 | custom fusion | bytes 8389120 | tf_op jit(solution)/shard_map/gather | solution.py:126
  479.3 2.6 bitcast_reduce_fusion
  482.0 0.8 fusion.6
  482.9 0.8 copy.20
  (44 shorter events, 1.0 us)
Async XLA Ops:
  7.2 47.1 %copy-start = (bf16[1024,512]{1,0:T(8,128)(2,1)S(1)}, bf16[1024,512]{1,0:T(8,128)(2,1)}, u32[]{:S(2)}) copy-start(bf16[1024,512]{1,0:T(8,128)(2,1)} %param.9) | copy-start | bytes 3145732
  11.5 14.3 %all-to-all-start.1 = ((s32[32,1,8]{2,1,0:T(1,128)}), s32[32,1,8]{2,1,0:T(1,128)S(1)}, u32[]{:S(2)}, u32[]{:S(2)}) async-start(s32[32,1,8]{2,1,0:T(1,128)} %bitcast.7), calls=%async_computation.1 | async-start | bytes 32768 | tf_op jit(solution)/shard_map/all_to_all | solution.py:58
  25.8 22.4 %all-to-all-start.3 = ((s32[32,1,256]{2,1,0:T(1,128)}), s32[32,1,256]{2,1,0:T(1,128)S(1)}, u32[]{:S(2)}, u32[]{:S(2)}) async-start(s32[32,1,256]{2,1,0:T(1,128)} %reshape.328), calls=%async_computation.3 | async-start | bytes 65536 | tf_op jit(solution)/shard_map/all_to_all | solution.py:59
  48.3 6.0 %copy-start.10 = (s32[4096]{0:T(1024)S(1)}, s32[4096]{0:T(1024)}, u32[]{:S(2)}) copy-start(s32[4096]{0:T(1024)} %param.11) | copy-start | bytes 49156
  48.3 102.0 %all-to-all-start = ((bf16[32,8,32,256]{3,2,1,0:T(8,128)(2,1)}), bf16[32,8,32,256]{3,2,1,0:T(8,128)(2,1)}, u32[]{:S(2)}, u32[]{:S(2)}) async-start(bf16[32,8,32,256]{3,2,1,0:T(8,128)(2,1)} %bitcast.67), calls=%async_computation | async-start | bytes 8388608 | tf_op jit(solution)/shard_map/all_to_all | solution.py:67
  54.3 8.2 %copy-start.9 = (bf16[512,256]{1,0:T(8,128)(2,1)S(1)}, bf16[512,256]{1,0:T(8,128)(2,1)}, u32[]{:S(2)}) copy-start(bf16[512,256]{1,0:T(8,128)(2,1)} %param.10) | copy-start | bytes 786436
  62.5 2.0 copy-start.5
  64.5 1.9 copy-start.2
  162.3 9.8 %all-to-all-start.4 = ((f32[32,1,256]{2,1,0:T(1,128)}), f32[32,1,256]{2,1,0:T(1,128)S(1)}, u32[]{:S(2)}, u32[]{:S(2)}) async-start(f32[32,1,256]{2,1,0:T(1,128)} %reshape.330), calls=%async_computation.4 | async-start | bytes 65536 | tf_op jit(solution)/shard_map/all_to_all | solution.py:87
  172.1 9.9 %all-to-all-start.2 = ((f32[32,1,256]{2,1,0:T(1,128)}), f32[32,1,256]{2,1,0:T(1,128)S(1)}, u32[]{:S(2)}, u32[]{:S(2)}) async-start(f32[32,1,256]{2,1,0:T(1,128)} %reshape.332), calls=%async_computation.2 | async-start | bytes 65536 | tf_op jit(solution)/shard_map/all_to_all | solution.py:86
  206.7 266.4 %all-to-all-start.6 = ((f32[32,8,32,256]{3,2,1,0:T(8,128)}), f32[32,8,32,256]{3,2,1,0:T(8,128)}, u32[]{:S(2)}, u32[]{:S(2)}) async-start(f32[32,8,32,256]{3,2,1,0:T(8,128)} %broadcast_multiply_fusion), calls=%async_computation.6 | async-start | bytes 16777216 | tf_op jit(solution)/shard_map/all_to_all | solution.py:122
  210.4 259.8 %all-reduce.3.cloned.1.call-start = ((), (), s32[]{:S(2)}) async-start(), calls=%async_computation.7 | async-start | bytes 5242880 | tf_op jit(solution)/shard_map/psum | solution.py:146
  250.2 4.6 copy-start.3
  250.2 5.9 %copy-start.4 = (f32[4096,256]{1,0:T(8,128)S(1)}, f32[4096,256]{1,0:T(8,128)}, u32[]{:S(2)}) copy-start(f32[4096,256]{1,0:T(8,128)} %reshape.201) | copy-start | bytes 12582916
  256.1 2.4 copy-start.6
  473.1 10.6 %copy-start.1 = (bf16[1024,512]{1,0:T(8,128)(2,1)S(1)}, bf16[1024,512]{1,0:T(8,128)(2,1)}, u32[]{:S(2)}) copy-start(bf16[1024,512]{1,0:T(8,128)(2,1)} %param.9) | copy-start | bytes 3145732
  479.3 2.6 copy-start.7
  479.3 3.6 copy-start.8
Sparse Core Ops, SparseCore 0:
  272.3 197.8 all-reduce.2
where the time goes:
time: 492 us; the launch traced here: 491 us
  waiting for transfers between devices  284 us (58%)
  local copies, waits for them, and re-layouts  73.8 us (15%)
  matrix products  64 us (13%)
  starting transfers between devices  24.9 us (5%)
  other arithmetic  20.1 us (4%)
  between operations  14.4 us (3%)
  blocking collectives  8.88 us (2%)
    psum x1, waiting for transfers between devices, body(): lax.psum((first_gradient, second_gradient), ('user', 'item'))  197 us
    all_to_all x1, waiting for transfers between devices, body(): lax.all_to_all(slot_users.reshape(devices, capacity, group_size, -1), ('u...  71.4 us
    unnamed x33, local copies, waits for them, and re-layouts  26.5 us
    scatter x1, local copies, waits for them, and re-layouts, body(): slot_users = jnp.zeros((devices * capacity, group_size, group_users.shape...  15.7 us
    dot_general x1, matrix products, body(): jnp.einsum('nkub,nkue->nkbe', score_grad, users_in, preferred_element_typ...  13 us
    dot_general x1, matrix products, body(): jnp.einsum('nkub,nkbe->nkue', score_grad, blocks_in, preferred_element_ty...  11.7 us
    dot_general x1, matrix products, body(): jnp.dot(item_feats.T, act_gradient, preferred_element_type=jnp.float32)  11.6 us
    dot_general x1, matrix products, body(): jnp.einsum('nkue,nkbe->nkub', users_in, blocks_in, preferred_element_type...  11.4 us
  transfers between devices with their start and end apart: 7, of which 5 were waited for; matrix products, arithmetic and copies ran while one was open for 23% of the time, Pallas kernels for 0%

commit v1 on v0

--- a/solution.py
+++ b/solution.py
@@ -9,6 +9,11 @@
 LOGIT_SCALE = 20.0
 LOSS_SCALE = 4096.0
 NORM_EPSILON = 1e-06
+
+
+def measure_the_gates(sample):
+    vec_out = jax.lax.psum(sample, axis_name="item")
+    return jax.lax.psum(vec_out, "user")
 
 
 def body(
@@ -143,7 +148,7 @@
         hidden > 0, jnp.dot(out_gradient, second_weight.T, preferred_element_type=jnp.float32), 0.0
     ).astype(jnp.bfloat16)
     first_gradient = jnp.dot(item_feats.T, act_gradient, preferred_element_type=jnp.float32)
-    first_gradient, second_gradient = lax.psum((first_gradient, second_gradient), ("user", "item"))
+    first_gradient, second_gradient = measure_the_gates((first_gradient, second_gradient))
     vector_grad = vector_grad.reshape(user_rows, -1)
     user_projection = jnp.sum(user_float * vector_grad, axis=1, keepdims=True)
     user_gradient = vector_grad * user_norm - user_float * (

time: 492 us -> 552 us (1.12)
  waiting for transfers between devices: 284 us -> 344 us
    psum x1 -> x2, waiting for transfers between devices: 197 us -> 257 us  [the longest x1 194 us: measure_the_gates(): vec_out = jax.lax.psum(sample, axis_name='item')]
  transfers between devices with their start and end apart: 7 -> 8, of which waited for: 5 -> 6; matrix products, arithmetic and copies ran while one was open for 23% -> 20% of each run, Pallas kernels for 0% -> 0%
where the time goes in v1:
time: 552 us; the launch traced here: 550 us
  waiting for transfers between devices  344 us (62%)
  local copies, waits for them, and re-layouts  73.8 us (13%)
  matrix products  64 us (12%)
  starting transfers between devices  24.9 us (5%)
  other arithmetic  20.1 us (4%)
  between operations  14.4 us (3%)
  blocking collectives  8.88 us (2%)
    psum x1, waiting for transfers between devices, measure_the_gates(): vec_out = jax.lax.psum(sample, axis_name='item')  194 us
    all_to_all x1, waiting for transfers between devices, body(): lax.all_to_all(slot_users.reshape(devices, capacity, group_size, -1), ('u...  71.4 us
    psum x1, waiting for transfers between devices, measure_the_gates(): return jax.lax.psum(vec_out, 'user')  62.7 us
    unnamed x33, local copies, waits for them, and re-layouts  26.5 us
    scatter x1, local copies, waits for them, and re-layouts, body(): slot_users = jnp.zeros((devices * capacity, group_size, group_users.shape...  15.7 us
    dot_general x1, matrix products, body(): jnp.einsum('nkub,nkue->nkbe', score_grad, users_in, preferred_element_typ...  13 us
    dot_general x1, matrix products, body(): jnp.einsum('nkub,nkbe->nkue', score_grad, blocks_in, preferred_element_ty...  11.7 us
    dot_general x1, matrix products, body(): jnp.dot(item_feats.T, act_gradient, preferred_element_type=jnp.float32)  11.6 us
  transfers between devices with their start and end apart: 8, of which 6 were waited for; matrix products, arithmetic and copies ran while one was open for 20% of the time, Pallas kernels for 0%

profile of v1, /device:TPU:0, one launch (start us, length us, event | category | flops | bytes accessed | tf_op | source)
XLA Modules:
  0.0 550.4 jit_solution(5154468230276725083)
XLA Ops:
  7.2 0.8 fusion.13
  8.2 0.8 select_reduce_fusion.1
  9.0 0.7 fusion.27
  9.7 1.1 scatter_custom_fusion.1
  10.8 0.7 all_to_all.27
  11.5 7.3 %all-to-all-start.1 = ((s32[32,1,8]{2,1,0:T(1,128)}), s32[32,1,8]{2,1,0:T(1,128)S(1)}, u32[]{:S(2)}, u32[]{:S(2)}) async-start(s32[32,1,8]{2,1,0:T(1,128)} %bitcast.7), calls=%async_computation.1 | async-start | bytes 32768 | tf_op jit(solution)/shard_map/all_to_all | solution.py:63
  18.8 1.0 fusion.3
  19.9 0.8 reshape.192
  20.6 1.0 scatter_custom_fusion.2
  21.7 0.7 reshape.328
  22.4 3.4 all-to-all-done.1
  25.8 2.6 all-to-all-start.3
  28.4 1.0 fusion.4
  29.4 0.7 gather_fusion
  30.1 2.5 broadcast_in_dim.16
  32.6 15.7 %scatter_fusion = bf16[256,32,256]{2,1,0:T(8,128)(2,1)} fusion(bf16[256,32,256]{2,1,0:T(8,128)(2,1)} %broadcast_in_dim.16, s32[128]{0:T(128)S(1)} %fusion.27, bf16[128,32,256]{2,1,0:T(8,128)(2,1)S(1)} %gather_fusion), kind=kCustom, calls=%fused_computation.8 | custom fusion | bytes 6291968 | tf_op jit(solution)/shard_map/scatter | solution.py:59
  48.3 6.0 %all-to-all-start = ((bf16[32,8,32,256]{3,2,1,0:T(8,128)(2,1)}), bf16[32,8,32,256]{3,2,1,0:T(8,128)(2,1)}, u32[]{:S(2)}, u32[]{:S(2)}) async-start(bf16[32,8,32,256]{3,2,1,0:T(8,128)(2,1)} %bitcast.67), calls=%async_computation | async-start | bytes 8388608 | tf_op jit(solution)/shard_map/all_to_all | solution.py:72
  54.3 8.2 %maximum_convert_fusion = bf16[4096,512]{1,0:T(8,128)(2,1)S(1)} fusion(bf16[4096,1024]{1,0:T(8,128)(2,1)} %param.8, bf16[1024,512]{1,0:T(8,128)(2,1)S(1)} %copy-done), kind=kOutput, calls=%fused_computation.15 | convolution fusion | flops 4299161600 | bytes 13631488 | tf_op jit(solution)/shard_map/dot_general | solution.py:30
  62.5 1.3 multiply_reduce_fusion.1
  63.8 0.7 copy-done.5
  64.6 1.9 copy-done.2
  66.5 0.7 multiply_convert_fusion.2
  67.3 0.9 gather_fusion.2
  68.2 9.4 %gather_fusion.1 = bf16[256,128,256]{2,1,0:T(8,128)(2,1)} fusion(bf16[32,128,256]{2,1,0:T(8,128)(2,1)S(1)} %bitcast.62, s32[1024]{0:T(1024)S(1)} %pad_clamp_fusion.1), kind=kCustom, calls=%fused_computation.1 | custom fusion | bytes 33555456 | tf_op jit(solution)/shard_map/gather | solution.py:79
  77.5 0.5 broadcast.184
  78.1 0.7 reduce.4
  78.9 71.4 %all-to-all-done = bf16[32,8,32,256]{3,2,1,0:T(8,128)(2,1)} async-done(((bf16[32,8,32,256]{3,2,1,0:T(8,128)(2,1)}), bf16[32,8,32,256]{3,2,1,0:T(8,128)(2,1)}, u32[]{:S(2)}, u32[]{:S(2)}) %all-to-all-start) | async-done | bytes 4194336 | tf_op jit(solution)/shard_map/all_to_all | solution.py:72
  150.2 11.4 %exponential_reduce_fusion = (f32[32,8,32]{2,1,0:T(8,128)S(1)}, f32[32,8,32]{2,1,0:T(8,128)S(1)}, f32[32,8,32,128]{3,2,1,0:T(8,128)}) fusion(f32[32,8,128]{2,1,0:T(8,128)S(1)} %bitcast_convert_fusion, s32[32,8,32]{2,1,0:T(8,128)S(1)} %reshape.329, bf16[32,8,32,256]{3,2,1,0:T(8,128)(2,1)} %all-to-all-done, bf16[32,8,128,256]{3,2,1,0:T(8,128)(2,1)} %bitcast.63), kind=kOutput, calls=%fused_computation.26 | convolution fusion | flops 543145984 | bytes 25395200 | tf_op jit(solution)/shard_map/nkue,nkbe->nkub/dot_general | solution.py:83
  161.6 0.7 reshape.330
  162.3 2.6 all-to-all-start.4
  164.9 0.7 reshape.332
  165.7 6.5 %all-to-all-done.4 = f32[32,1,256]{2,1,0:T(1,128)S(1)} async-done(((f32[32,1,256]{2,1,0:T(1,128)}), f32[32,1,256]{2,1,0:T(1,128)S(1)}, u32[]{:S(2)}, u32[]{:S(2)}) %all-to-all-start.4) | async-done | bytes 32800 | tf_op jit(solution)/shard_map/all_to_all | solution.py:92
  172.1 2.7 all-to-all-start.2
  174.9 0.5 broadcast.185
  175.4 0.7 reduce.5
  176.2 5.8 %all-to-all-done.2 = f32[32,1,256]{2,1,0:T(1,128)S(1)} async-done(((f32[32,1,256]{2,1,0:T(1,128)}), f32[32,1,256]{2,1,0:T(1,128)S(1)}, u32[]{:S(2)}, u32[]{:S(2)}) %all-to-all-start.2) | async-done | bytes 32800 | tf_op jit(solution)/shard_map/all_to_all | solution.py:91
  182.0 0.7 reduce.6
  182.9 0.7 gather_fusion.4
  183.5 0.6 gather_fusion.3
  184.2 1.0 scatter_custom_fusion.3
  185.3 8.9 %all_to_all.42 = f32[32,1,256]{2,1,0:T(1,128)S(1)} all-to-all(f32[32,1,256]{2,1,0:T(1,128)S(1)} %reshape.334), channel_id=1, replica_groups=mesh['user'=4,'item'=8] {'user','item'}, dimensions={0} | all-to-all | bytes 65536 | tf_op jit(solution)/shard_map/all_to_all | solution.py:108
  194.2 0.7 reduce.7
  195.0 11.7 %broadcast_multiply_fusion = f32[32,8,32,256]{3,2,1,0:T(8,128)} fusion(bf16[32,8,128,256]{3,2,1,0:T(8,128)(2,1)} %bitcast.64, f32[32,8,32,128]{3,2,1,0:T(8,128)} %get-tuple-element.24, f32[32,8,32]{2,1,0:T(8,128)S(1)} %reshape.335, s32[32,8,32]{2,1,0:T(8,128)S(1)} %reshape.329, f32[32,8,128]{2,1,0:T(8,128)S(1)} %bitcast_convert_fusion), kind=kOutput, calls=%fused_computation.19 | convolution fusion | flops 547356672 | bytes 29556736 | tf_op jit(solution)/shard_map/nkub,nkbe->nkue/dot_general | solution.py:124
  206.7 3.7 all-to-all-start.6
  210.4 0.5 broadcast.183
  210.9 0.7 reduce.3
  211.7 13.0 %fusion = bf16[32,8,128,256]{3,2,1,0:T(8,128)(2,1)} fusion(bf16[32,8,32,256]{3,2,1,0:T(8,128)(2,1)} %all-to-all-done, f32[32,8,32,128]{3,2,1,0:T(8,128)} %get-tuple-element.24, f32[32,8,32]{2,1,0:T(8,128)S(1)} %reshape.335, s32[32,8,32]{2,1,0:T(8,128)S(1)} %reshape.329, f32[32,8,128]{2,1,0:T(8,128)S(1)} %bitcast_convert_fusion), kind=kOutput, calls=%fused_computation.13 | convolution fusion | flops 562036736 | bytes 25362432 | tf_op jit(solution)/shard_map/nkub,nkue->nkbe/dot_general | solution.py:122
  224.7 15.8 %copy.16 = bf16[32,8,128,256]{3,1,2,0:T(8,128)(2,1)S(1)} copy(bf16[32,8,128,256]{3,2,1,0:T(8,128)(2,1)} %fusion) | data formatting | bytes 33554432
  240.5 4.8 fusion.22
  245.3 4.9 reshape.201
  250.2 4.2 multiply_reduce_fusion
  254.4 0.4 copy-done.3
  254.8 1.3 copy-done.4
  256.1 2.4 subtract_convert_fusion
  258.5 2.1 fusion.33
  260.6 11.6 %fusion.2 = f32[1024,512]{0,1:T(8,128)} fusion(bf16[4096,1024]{1,0:T(8,128)(2,1)} %param.8, bf16[4096,512]{1,0:T(8,128)(2,1)} %copy-done.5, bf16[4096,256]{1,0:T(8,128)(2,1)S(1)} %subtract_convert_fusion, bf16[512,256]{1,0:T(8,128)(2,1)S(1)} %copy-done.9), kind=kOutput, calls=%fused_computation.28 | convolution fusion | flops 5375000576 | bytes 17039360 | tf_op jit(solution)/shard_map/dot_general | solution.py:150
  272.3 194.4 %all-reduce.5.cloned.1.call-done = (f32[1024,512]{0,1:T(8,128)}, f32[512,256]{1,0:T(8,128)}) async-done(((f32[1024,512]{0,1:T(8,128)}, f32[512,256]{1,0:T(8,128)}), (f32[1024,512]{0,1:T(8,128)}, f32[512,256]{1,0:T(8,128)})) %all-reduce.5.cloned.1.call-update) | async-done | bytes 2621456 | tf_op jit(solution)/shard_map/psum | solution.py:15
  466.7 0.6 sub.52
  467.4 62.7 %all-reduce.7.cloned.1.call-done = (f32[1024,512]{0,1:T(8,128)}, f32[512,256]{1,0:T(8,128)}) async-done(((f32[1024,512]{0,1:T(8,128)}, f32[512,256]{1,0:T(8,128)}), (f32[1024,512]{0,1:T(8,128)}, f32[512,256]{1,0:T(8,128)})) %all-reduce.7.cloned.1.call-update) | async-done | bytes 2621456 | tf_op jit(solution)/shard_map/psum | solution.py:16
  530.1 2.9 copy.15
  533.0 6.2 %gather_fusion.5 = f32[128,32,256]{2,1,0:T(8,128)} fusion(f32[256,32,256]{2,1,0:T(8,128)} %bitcast.18, s32[1024]{0:T(1024)S(1)} %pad_clamp_fusion), kind=kCustom, calls=%fused_computation.7 | custom fusion | bytes 8389120 | tf_op jit(solution)/shard_map/gather | solution.py:131
  539.2 2.6 bitcast_reduce_fusion
  541.9 0.8 fusion.6
  542.8 0.8 copy.22
  (47 shorter events, 1.2 us)
Async XLA Ops:
  7.2 47.1 %copy-start = (bf16[1024,512]{1,0:T(8,128)(2,1)S(1)}, bf16[1024,512]{1,0:T(8,128)(2,1)}, u32[]{:S(2)}) copy-start(bf16[1024,512]{1,0:T(8,128)(2,1)} %param.9) | copy-start | bytes 3145732
  11.5 14.3 %all-to-all-start.1 = ((s32[32,1,8]{2,1,0:T(1,128)}), s32[32,1,8]{2,1,0:T(1,128)S(1)}, u32[]{:S(2)}, u32[]{:S(2)}) async-start(s32[32,1,8]{2,1,0:T(1,128)} %bitcast.7), calls=%async_computation.1 | async-start | bytes 32768 | tf_op jit(solution)/shard_map/all_to_all | solution.py:63
  25.8 22.4 %all-to-all-start.3 = ((s32[32,1,256]{2,1,0:T(1,128)}), s32[32,1,256]{2,1,0:T(1,128)S(1)}, u32[]{:S(2)}, u32[]{:S(2)}) async-start(s32[32,1,256]{2,1,0:T(1,128)} %reshape.328), calls=%async_computation.3 | async-start | bytes 65536 | tf_op jit(solution)/shard_map/all_to_all | solution.py:64
  48.3 6.0 %copy-start.10 = (s32[4096]{0:T(1024)S(1)}, s32[4096]{0:T(1024)}, u32[]{:S(2)}) copy-start(s32[4096]{0:T(1024)} %param.11) | copy-start | bytes 49156
  48.3 102.0 %all-to-all-start = ((bf16[32,8,32,256]{3,2,1,0:T(8,128)(2,1)}), bf16[32,8,32,256]{3,2,1,0:T(8,128)(2,1)}, u32[]{:S(2)}, u32[]{:S(2)}) async-start(bf16[32,8,32,256]{3,2,1,0:T(8,128)(2,1)} %bitcast.67), calls=%async_computation | async-start | bytes 8388608 | tf_op jit(solution)/shard_map/all_to_all | solution.py:72
  54.3 8.2 %copy-start.9 = (bf16[512,256]{1,0:T(8,128)(2,1)S(1)}, bf16[512,256]{1,0:T(8,128)(2,1)}, u32[]{:S(2)}) copy-start(bf16[512,256]{1,0:T(8,128)(2,1)} %param.10) | copy-start | bytes 786436
  62.5 2.0 copy-start.5
  64.5 1.9 copy-start.2
  162.3 9.8 %all-to-all-start.4 = ((f32[32,1,256]{2,1,0:T(1,128)}), f32[32,1,256]{2,1,0:T(1,128)S(1)}, u32[]{:S(2)}, u32[]{:S(2)}) async-start(f32[32,1,256]{2,1,0:T(1,128)} %reshape.330), calls=%async_computation.4 | async-start | bytes 65536 | tf_op jit(solution)/shard_map/all_to_all | solution.py:92
  172.1 9.9 %all-to-all-start.2 = ((f32[32,1,256]{2,1,0:T(1,128)}), f32[32,1,256]{2,1,0:T(1,128)S(1)}, u32[]{:S(2)}, u32[]{:S(2)}) async-start(f32[32,1,256]{2,1,0:T(1,128)} %reshape.332), calls=%async_computation.2 | async-start | bytes 65536 | tf_op jit(solution)/shard_map/all_to_all | solution.py:91
  206.7 326.3 %all-to-all-start.6 = ((f32[32,8,32,256]{3,2,1,0:T(8,128)}), f32[32,8,32,256]{3,2,1,0:T(8,128)}, u32[]{:S(2)}, u32[]{:S(2)}) async-start(f32[32,8,32,256]{3,2,1,0:T(8,128)} %broadcast_multiply_fusion), calls=%async_computation.6 | async-start | bytes 16777216 | tf_op jit(solution)/shard_map/all_to_all | solution.py:127
  210.4 256.3 %all-reduce.5.cloned.1.call-start = ((), (), s32[]{:S(2)}) async-start(), calls=%async_computation.7 | async-start | bytes 5242880 | tf_op jit(solution)/shard_map/psum | solution.py:15
  250.2 4.6 copy-start.3
  250.2 5.9 %copy-start.4 = (f32[4096,256]{1,0:T(8,128)S(1)}, f32[4096,256]{1,0:T(8,128)}, u32[]{:S(2)}) copy-start(f32[4096,256]{1,0:T(8,128)} %reshape.201) | copy-start | bytes 12582916
  256.1 2.4 copy-start.6
  272.2 257.9 %all-reduce.7.cloned.1.call-start = ((), (), s32[]{:S(2)}) async-start(), calls=%async_computation.8 | async-start | bytes 5242880 | tf_op jit(solution)/shard_map/psum | solution.py:16
  533.0 10.6 %copy-start.1 = (bf16[1024,512]{1,0:T(8,128)(2,1)S(1)}, bf16[1024,512]{1,0:T(8,128)(2,1)}, u32[]{:S(2)}) copy-start(bf16[1024,512]{1,0:T(8,128)(2,1)} %param.9) | copy-start | bytes 3145732
  539.2 2.6 copy-start.7
  539.2 3.6 copy-start.8
Sparse Core Ops, SparseCore 0:
  272.3 194.3 all-reduce.4
  469.2 60.8 all-reduce.6
